TPU v7x, 512 devices: a whole 4x8x8 slice. The times are simulated.
512 devices in a mesh: clip: 64 (over z, y_hi, x), val: 8 (over y_lo, core).
Axes of the slice: x: 4, y: 8 (y_hi: 2, y_lo: 4; y = y_hi * 4 + y_lo), z: 8, core: 2. Of those that a mesh axis runs over, the one named last changes fastest.
Arguments:
- latents: bfloat16 [1024, 8192], P('clip', 'val'), may hold values from -10 to 10
- noise: bfloat16 [1024, 8192], P('clip', 'val'), may hold values from -10 to 10
- offsets: int32 [1024, 2, 2], P('clip'), may hold values from 0 to 15
- times: float32 [1024], P('clip'), may hold values from 0.05 to 0.95
- embed: bfloat16 [64, 5120], replicated, may hold values from -0.75 to 0.75
Outputs:
- embedded: bfloat16 [1024, 128, 5120], P('clip', 'val')
All inputs are finite; a program needn't handle non-finite values.
Results may differ from a plain program's by a relative error of at most 0.0051.
Values may be sent and summed in bfloat16 or wider, within the bound.
A program may use at most 64 MiB of HBM per device.

v0:
```python
import math
import jax
import jax.numpy as jnp
from jax import lax
from jax.sharding import PartitionSpec as P

P_SIZE = 64
FR = 2
GW = 16
GH = 4
ITERS = 4
S = 128


def warp_noise(noise, offsets):
    clips = noise.shape[0]
    tokens = FR * GH * GW
    value_cube = noise.reshape(clips, noise.shape[1] // tokens, tokens)
    shift_y = offsets[:, :, 0] % GH
    shift_x = offsets[:, :, 1] % GW
    src_rows = (jnp.arange(GH, dtype=jnp.int32)[None, None, :] - shift_y[:, :, None]) % GH
    src_cols = (jnp.arange(GW, dtype=jnp.int32)[None, None, :] - shift_x[:, :, None]) % GW
    frame_base = (jnp.arange(FR, dtype=jnp.int32) * (GH * GW))[None, :, None, None]
    source = (frame_base + src_rows[:, :, :, None] * GW + src_cols[:, :, None, :]).reshape(
        clips, tokens
    )
    source = jnp.broadcast_to(source[:, None, :], value_cube.shape)
    return jnp.take_along_axis(value_cube, source, axis=2).reshape(noise.shape)


def row_stats(scores):
    top = jnp.max(scores, axis=1)
    total = jnp.sum(jnp.exp(scores - top[:, None]), axis=1)
    return (top, total)


def column_lse(scores):
    top = jnp.max(scores, axis=0)
    top = lax.pmax(top, "clip")
    total = lax.psum(jnp.sum(jnp.exp(scores - top[None, :]), axis=0), "clip")
    return top + jnp.log(total)


def on_device(latents, noise, offsets, times, embed):
    warped = warp_noise(noise, offsets)
    clips = latents.shape[0]
    volume = P_SIZE * S
    entropy = 0.5 / math.sqrt(volume)
    contract = (((1,), (1,)), ((), ()))
    panel_all = lax.all_gather(warped, "clip", axis=0, tiled=True)
    gram_part = lax.dot_general(latents, panel_all, contract, preferred_element_type=jnp.float32)
    square_part = jnp.sum(jnp.square(panel_all.astype(jnp.float32)), axis=1)
    gram, square = lax.psum((gram_part, square_part), "val")
    cost = (square[None, :] - 2.0 * gram) / volume
    column_dual = jnp.zeros((cost.shape[1],), jnp.float32)
    for sweep_index in range(ITERS):
        top, total = row_stats((column_dual[None, :] - cost) / entropy)
        row_dual = -entropy * (top + jnp.log(total))
        column_dual = -entropy * column_lse((row_dual[:, None] - cost) / entropy)
    scores = (column_dual[None, :] - cost) / entropy
    top, total = row_stats(scores)
    weights = (jnp.exp(scores - top[:, None]) / total[:, None]).astype(jnp.bfloat16)
    coupled = jnp.dot(weights, panel_all, preferred_element_type=jnp.float32)
    mixed = (
        (1.0 - times)[:, None] * latents.astype(jnp.float32) + times[:, None] * coupled
    ).astype(jnp.bfloat16)
    value_cube = mixed.reshape(clips, latents.shape[1] // S, S)
    return jnp.einsum(
        "cps,pd->csd",
        lax.all_to_all(value_cube, "val", split_axis=2, concat_axis=1, tiled=True),
        embed,
        preferred_element_type=jnp.float32,
    ).astype(jnp.bfloat16)


def solution(mesh):
    placed = (P("clip", "val"), P("clip", "val"), P("clip", None, None), P("clip"), P())
    return jax.shard_map(
        on_device, mesh=mesh, in_specs=placed, out_specs=P("clip", "val", None), check_vma=False
    )
```

profile of v0, /device:TPU:1, one launch (start us, length us, event | category | flops | bytes accessed | tf_op | source)
XLA Modules:
  0.0 2139.3 jit_solution(8296339982809576350)
XLA Ops:
  8.7 145.1 %gather_fusion = bf16[16384]{0:T(1024)(128)(2,1)S(1)} fusion(bf16[16,8,128]{2,1,0:T(8,128)(2,1)S(1)} %bitcast.32, s32[16384]{0:T(1024)S(1)} %or_bitcast_fusion), kind=kCustom, calls=%fused_computation | custom fusion | bytes 262144 | tf_op jit(solution)/shard_map/jit(take_along_axis)/gather | solution.py:28
  154.6 135.1 %all-gather.2.cloned.1.call-done = bf16[1024,1024]{1,0:T(8,128)(2,1)} async-done(((bf16[16,1024]{1,0:T(8,128)(2,1)}), bf16[1024,1024]{1,0:T(8,128)(2,1)}) %all-gather.2.cloned.1.call-update) | async-done | bytes 2097168 | tf_op jit(solution)/shard_map/all_gather | solution.py:50
  289.7 3.0 convolution_bitcast_fusion
  293.3 17.5 psum.42
  310.8 55.7 %all-reduce.2.cloned.1.call-done = f32[16,1024]{1,0:T(8,128)} async-done(((f32[16,1024]{1,0:T(8,128)}), f32[16,1024]{1,0:T(8,128)}) %all-reduce.2.cloned.1.call-update) | async-done | bytes 65552 | tf_op jit(solution)/shard_map/psum | solution.py:53
  367.5 1.0 exponential_reduce_fusion.7
  369.4 197.3 %pmax.28 = f32[1024]{0:T(1024)S(1)} all-reduce(f32[1024]{0:T(1024)S(1)} %fusion.8), channel_id=1, replica_groups=mesh['clip'=64,'val'=8] {'clip'}, use_global_device_ids=true, to_apply=%region_6.7 | all-reduce | flops 1024 | bytes 8192 | tf_op jit(solution)/shard_map/pmax | solution.py:39
  567.6 187.5 %psum.44 = f32[1024]{0:T(1024)S(1)} all-reduce(f32[1024]{0:T(1024)S(1)} %exponential_reduce_fusion.6), channel_id=1, replica_groups=mesh['clip'=64,'val'=8] {'clip'}, use_global_device_ids=true, to_apply=%region_8.9 | all-reduce | flops 1024 | bytes 8192 | tf_op jit(solution)/shard_map/psum | solution.py:40
  755.2 1.0 fusion.9
  756.1 1.0 exponential_reduce_fusion.5
  758.1 188.7 %pmax.29 = f32[1024]{0:T(1024)S(1)} all-reduce(f32[1024]{0:T(1024)S(1)} %fusion.10), channel_id=1, replica_groups=mesh['clip'=64,'val'=8] {'clip'}, use_global_device_ids=true, to_apply=%region_12.13 | all-reduce | flops 1024 | bytes 8192 | tf_op jit(solution)/shard_map/pmax | solution.py:39
  947.8 187.4 %psum.45 = f32[1024]{0:T(1024)S(1)} all-reduce(f32[1024]{0:T(1024)S(1)} %exponential_reduce_fusion.4), channel_id=1, replica_groups=mesh['clip'=64,'val'=8] {'clip'}, use_global_device_ids=true, to_apply=%region_14.15 | all-reduce | flops 1024 | bytes 8192 | tf_op jit(solution)/shard_map/psum | solution.py:40
  1135.1 1.0 fusion.11
  1136.1 1.0 exponential_reduce_fusion.3
  1138.1 189.1 %pmax.30 = f32[1024]{0:T(1024)S(1)} all-reduce(f32[1024]{0:T(1024)S(1)} %fusion.12), channel_id=1, replica_groups=mesh['clip'=64,'val'=8] {'clip'}, use_global_device_ids=true, to_apply=%region_18.19 | all-reduce | flops 1024 | bytes 8192 | tf_op jit(solution)/shard_map/pmax | solution.py:39
  1328.2 187.5 %psum.46 = f32[1024]{0:T(1024)S(1)} all-reduce(f32[1024]{0:T(1024)S(1)} %exponential_reduce_fusion.2), channel_id=1, replica_groups=mesh['clip'=64,'val'=8] {'clip'}, use_global_device_ids=true, to_apply=%region_20.21 | all-reduce | flops 1024 | bytes 8192 | tf_op jit(solution)/shard_map/psum | solution.py:40
  1515.7 1.0 fusion.13
  1516.7 1.0 exponential_reduce_fusion.1
  1518.7 189.0 %pmax.31 = f32[1024]{0:T(1024)S(1)} all-reduce(f32[1024]{0:T(1024)S(1)} %fusion.14), channel_id=1, replica_groups=mesh['clip'=64,'val'=8] {'clip'}, use_global_device_ids=true, to_apply=%region_24.25 | all-reduce | flops 1024 | bytes 8192 | tf_op jit(solution)/shard_map/pmax | solution.py:39
  1708.6 187.5 %psum.47 = f32[1024]{0:T(1024)S(1)} all-reduce(f32[1024]{0:T(1024)S(1)} %exponential_reduce_fusion), channel_id=1, replica_groups=mesh['clip'=64,'val'=8] {'clip'}, use_global_device_ids=true, to_apply=%region_26.27 | all-reduce | flops 1024 | bytes 8192 | tf_op jit(solution)/shard_map/psum | solution.py:40
  1897.1 1.0 fusion.16
  1898.1 1.3 fusion.2
  1899.9 229.7 %all_to_all.18 = bf16[8,2,1024]{2,1,0:T(2,128)(2,1)S(1)} all-to-all(bf16[8,2,1024]{2,1,0:T(2,128)(2,1)S(1)} %reshape.134), channel_id=1, replica_groups=mesh['clip'=64,'val'=8] {'val'}, dimensions={0} | all-to-all | bytes 65536 | tf_op jit(solution)/shard_map/all_to_all | solution.py:70
  2130.3 2.1 convolution_convert_fusion
  (51 shorter events, 14.1 us)
Async XLA Ops:
  6.5 2123.8 %copy-start = (bf16[64,5120]{1,0:T(8,128)(2,1)S(1)}, bf16[64,5120]{1,0:T(8,128)(2,1)}, u32[]{:S(2)}) copy-start(bf16[64,5120]{1,0:T(8,128)(2,1)} %param.9) | copy-start | bytes 1966084
  6.5 283.2 %all-gather.2.cloned.1.call-start = ((), (), s32[]{:S(2)}) async-start(), calls=%async_computation.1 | async-start | bytes 2129920 | tf_op jit(solution)/shard_map/all_gather | solution.py:50
  8.7 145.9 %copy-start.3 = (f32[16]{0:T(128)S(1)}, f32[16]{0:T(128)}, u32[]{:S(2)}) copy-start(f32[16]{0:T(128)} %param.8) | copy-start | bytes 196
  8.7 281.0 %copy-start.2 = (bf16[16,1024]{1,0:T(8,128)(2,1)S(1)}, bf16[16,1024]{1,0:T(8,128)(2,1)}, u32[]{:S(2)}) copy-start(bf16[16,1024]{1,0:T(8,128)(2,1)} %param.5) | copy-start | bytes 98308
  154.5 212.0 %all-reduce.2.cloned.1.call-start = ((), (), s32[]{:S(2)}) async-start(), calls=%async_computation.2 | async-start | bytes 131072 | tf_op jit(solution)/shard_map/psum | solution.py:53
  289.7 3.1 copy-start.1
Sparse Core Ops, SparseCore 0:
  154.7 135.0 all-gather.1
  292.9 73.5 all-reduce.1
where the time goes:
time: 2140 us
  blocking collectives  1760 us (82%)
  waiting for transfers between devices  191 us (9%)
  local copies, waits for them, and re-layouts  148 us (7%)
    pmax x4, blocking collectives, column_lse(): top = lax.pmax(top, 'clip')  764 us
    psum x4, blocking collectives, column_lse(): total = lax.psum(jnp.sum(jnp.exp(scores - top[None, :]), axis=0), 'clip')  750 us
    all_to_all x1, blocking collectives, on_device(): lax.all_to_all(value_cube, 'val', split_axis=2, concat_axis=1, tiled=True)  230 us
    gather x1, local copies, waits for them, and re-layouts, warp_noise(): return jnp.take_along_axis(value_cube, source, axis=2).reshape(noise.shape)  145 us
    all_gather x1, waiting for transfers between devices, on_device(): panel_all = lax.all_gather(warped, 'clip', axis=0, tiled=True)  135 us
    psum x1, waiting for transfers between devices, on_device(): gram, square = lax.psum((gram_part, square_part), 'val')  55.7 us
  transfers between devices with their start and end apart: 2, of which 2 were waited for; matrix products, arithmetic and copies ran while one was open for 0% of the time, Pallas kernels for 0%

commit v1 on v0

--- a/solution.py
+++ b/solution.py
@@ -47,7 +47,9 @@
     volume = P_SIZE * S
     entropy = 0.5 / math.sqrt(volume)
     contract = (((1,), (1,)), ((), ()))
-    panel_all = lax.all_gather(warped, "clip", axis=0, tiled=True)
+    panel_all = jnp.concatenate(
+        lax.all_to_all(jnp.stack([warped] * lax.axis_size("clip")), "clip", 0, 0), axis=0
+    )
     gram_part = lax.dot_general(latents, panel_all, contract, preferred_element_type=jnp.float32)
     square_part = jnp.sum(jnp.square(panel_all.astype(jnp.float32)), axis=1)
     gram, square = lax.psum((gram_part, square_part), "val")

time: 2140 us -> 2080 us (0.972)
  waiting for transfers between devices: 191 us -> 104 us
    all_gather x1 -> x0, waiting for transfers between devices: 135 us -> none  [on_device(): panel_all = lax.all_gather(warped, 'clip', axis=0, tiled=True)]
    all_to_all x0 -> x1, waiting for transfers between devices: none -> 49.2 us  [on_device(): lax.all_to_all(jnp.stack([warped] * lax.axis_size('clip')), 'clip', 0, 0)]
where the time goes in v1:
time: 2080 us; the launch traced here: 2070 us
  blocking collectives  1760 us (85%)
  local copies, waits for them, and re-layouts  149 us (7%)
  waiting for transfers between devices  104 us (5%)
    pmax x4, blocking collectives, column_lse(): top = lax.pmax(top, 'clip')  764 us
    psum x4, blocking collectives, column_lse(): total = lax.psum(jnp.sum(jnp.exp(scores - top[None, :]), axis=0), 'clip')  750 us
    all_to_all x1, blocking collectives, on_device(): lax.all_to_all(value_cube, 'val', split_axis=2, concat_axis=1, tiled=True)  230 us
    gather x1, local copies, waits for them, and re-layouts, warp_noise(): return jnp.take_along_axis(value_cube, source, axis=2).reshape(noise.shape)  145 us
    psum x1, waiting for transfers between devices, on_device(): gram, square = lax.psum((gram_part, square_part), 'val')  54.7 us
    all_to_all x1, waiting for transfers between devices, on_device(): lax.all_to_all(jnp.stack([warped] * lax.axis_size('clip')), 'clip', 0, 0)  49.2 us
  transfers between devices with their start and end apart: 2, of which 2 were waited for; matrix products, arithmetic and copies ran while one was open for 0% of the time, Pallas kernels for 0%

profile of v1, /device:TPU:1, one launch (start us, length us, event | category | flops | bytes accessed | tf_op | source)
XLA Modules:
  0.0 2073.6 jit_solution(15573309284947173162)
XLA Ops:
  8.7 145.1 %gather_fusion = bf16[16384]{0:T(1024)(128)(2,1)S(1)} fusion(bf16[16,8,128]{2,1,0:T(8,128)(2,1)S(1)} %bitcast.33, s32[16384]{0:T(1024)S(1)} %or_bitcast_fusion), kind=kCustom, calls=%fused_computation | custom fusion | bytes 262144 | tf_op jit(solution)/shard_map/jit(take_along_axis)/gather | solution.py:28
  153.9 1.6 stack.3
  155.5 19.7 all-to-all-start
  175.3 49.2 %all-to-all-done = bf16[64,16,1024]{2,1,0:T(8,128)(2,1)S(1)} async-done(((bf16[64,16,1024]{2,1,0:T(8,128)(2,1)}), bf16[64,16,1024]{2,1,0:T(8,128)(2,1)S(1)}, u32[]{:S(2)}, u32[]{:S(2)}) %all-to-all-start) | async-done | bytes 2097184 | tf_op jit(solution)/shard_map/all_to_all | solution.py:51
  224.5 1.3 convolution_bitcast_fusion
  226.3 19.7 psum.42
  246.1 54.7 %all-reduce.2.cloned.1.call-done = f32[16,1024]{1,0:T(8,128)} async-done(((f32[16,1024]{1,0:T(8,128)}), f32[16,1024]{1,0:T(8,128)}) %all-reduce.2.cloned.1.call-update) | async-done | bytes 65552 | tf_op jit(solution)/shard_map/psum | solution.py:55
  301.8 1.0 exponential_reduce_fusion.7
  303.7 197.3 %pmax.28 = f32[1024]{0:T(1024)S(1)} all-reduce(f32[1024]{0:T(1024)S(1)} %fusion.8), channel_id=1, replica_groups=mesh['clip'=64,'val'=8] {'clip'}, use_global_device_ids=true, to_apply=%region_6.7 | all-reduce | flops 1024 | bytes 8192 | tf_op jit(solution)/shard_map/pmax | solution.py:39
  501.9 187.5 %psum.44 = f32[1024]{0:T(1024)S(1)} all-reduce(f32[1024]{0:T(1024)S(1)} %exponential_reduce_fusion.6), channel_id=1, replica_groups=mesh['clip'=64,'val'=8] {'clip'}, use_global_device_ids=true, to_apply=%region_8.9 | all-reduce | flops 1024 | bytes 8192 | tf_op jit(solution)/shard_map/psum | solution.py:40
  690.4 1.0 exponential_reduce_fusion.5
  692.4 188.7 %pmax.29 = f32[1024]{0:T(1024)S(1)} all-reduce(f32[1024]{0:T(1024)S(1)} %fusion.10), channel_id=1, replica_groups=mesh['clip'=64,'val'=8] {'clip'}, use_global_device_ids=true, to_apply=%region_12.13 | all-reduce | flops 1024 | bytes 8192 | tf_op jit(solution)/shard_map/pmax | solution.py:39
  882.0 187.4 %psum.45 = f32[1024]{0:T(1024)S(1)} all-reduce(f32[1024]{0:T(1024)S(1)} %exponential_reduce_fusion.4), channel_id=1, replica_groups=mesh['clip'=64,'val'=8] {'clip'}, use_global_device_ids=true, to_apply=%region_14.15 | all-reduce | flops 1024 | bytes 8192 | tf_op jit(solution)/shard_map/psum | solution.py:40
  1070.4 1.0 exponential_reduce_fusion.3
  1072.4 189.1 %pmax.30 = f32[1024]{0:T(1024)S(1)} all-reduce(f32[1024]{0:T(1024)S(1)} %fusion.12), channel_id=1, replica_groups=mesh['clip'=64,'val'=8] {'clip'}, use_global_device_ids=true, to_apply=%region_18.19 | all-reduce | flops 1024 | bytes 8192 | tf_op jit(solution)/shard_map/pmax | solution.py:39
  1262.5 187.5 %psum.46 = f32[1024]{0:T(1024)S(1)} all-reduce(f32[1024]{0:T(1024)S(1)} %exponential_reduce_fusion.2), channel_id=1, replica_groups=mesh['clip'=64,'val'=8] {'clip'}, use_global_device_ids=true, to_apply=%region_20.21 | all-reduce | flops 1024 | bytes 8192 | tf_op jit(solution)/shard_map/psum | solution.py:40
  1450.0 1.0 fusion.13
  1451.0 1.0 exponential_reduce_fusion.1
  1453.0 189.0 %pmax.31 = f32[1024]{0:T(1024)S(1)} all-reduce(f32[1024]{0:T(1024)S(1)} %fusion.14), channel_id=1, replica_groups=mesh['clip'=64,'val'=8] {'clip'}, use_global_device_ids=true, to_apply=%region_24.25 | all-reduce | flops 1024 | bytes 8192 | tf_op jit(solution)/shard_map/pmax | solution.py:39
  1642.9 187.5 %psum.47 = f32[1024]{0:T(1024)S(1)} all-reduce(f32[1024]{0:T(1024)S(1)} %exponential_reduce_fusion), channel_id=1, replica_groups=mesh['clip'=64,'val'=8] {'clip'}, use_global_device_ids=true, to_apply=%region_26.27 | all-reduce | flops 1024 | bytes 8192 | tf_op jit(solution)/shard_map/psum | solution.py:40
  1831.3 1.0 fusion.16
  1832.4 1.3 fusion.2
  1834.2 229.7 %all_to_all.23 = bf16[8,2,1024]{2,1,0:T(2,128)(2,1)S(1)} all-to-all(bf16[8,2,1024]{2,1,0:T(2,128)(2,1)S(1)} %reshape.143), channel_id=1, replica_groups=mesh['clip'=64,'val'=8] {'val'}, dimensions={0} | all-to-all | bytes 65536 | tf_op jit(solution)/shard_map/all_to_all | solution.py:72
  2064.6 2.1 convolution_convert_fusion
  (50 shorter events, 15.5 us)
Async XLA Ops:
  6.5 2058.1 %copy-start = (bf16[64,5120]{1,0:T(8,128)(2,1)S(1)}, bf16[64,5120]{1,0:T(8,128)(2,1)}, u32[]{:S(2)}) copy-start(bf16[64,5120]{1,0:T(8,128)(2,1)} %param.9) | copy-start | bytes 1966084
  155.5 19.8 copy-start.2
  155.5 69.0 %copy-start.1 = (bf16[16,1024]{1,0:T(8,128)(2,1)S(1)}, bf16[16,1024]{1,0:T(8,128)(2,1)}, u32[]{:S(2)}) copy-start(bf16[16,1024]{1,0:T(8,128)(2,1)} %param.5) | copy-start | bytes 98308
  155.5 69.0 %all-to-all-start = ((bf16[64,16,1024]{2,1,0:T(8,128)(2,1)}), bf16[64,16,1024]{2,1,0:T(8,128)(2,1)S(1)}, u32[]{:S(2)}, u32[]{:S(2)}) async-start(bf16[64,16,1024]{2,1,0:T(8,128)(2,1)} %stack.3), calls=%async_computation | async-start | bytes 4194304 | tf_op jit(solution)/shard_map/all_to_all | solution.py:51
  175.2 125.6 %all-reduce.2.cloned.1.call-start = ((), (), s32[]{:S(2)}) async-start(), calls=%async_computation.2 | async-start | bytes 131072 | tf_op jit(solution)/shard_map/psum | solution.py:55
Sparse Core Ops, SparseCore 0:
  225.9 74.8 all-reduce.1
